TPU v7x, 32 devices: a whole 2x2x4 slice. The times are simulated.
32 devices in a mesh: section: 4 (over y, core), expert: 4 (over z), mp: 2 (over x).
Axes of the slice: x: 2, y: 2, z: 4, core: 2. Of those that a mesh axis runs over, the one named last changes fastest.
Arguments:
- grad_top: bfloat16 [4, 64, 4096], P(None, 'expert', 'mp'), may hold values from -6 to 6
- w_down: bfloat16 [4, 4, 4096, 4096], P('section', 'expert', None, 'mp'), may hold values from -0.09375 to 0.09375
- w_up: bfloat16 [4, 4, 4096, 4096], P('section', 'expert', 'mp'), may hold values from -0.125 to 0.125
- saved: bfloat16 [4, 4, 4, 16, 4096], P('section', None, 'expert'), may hold values from -6 to 6
- assign: int32 [4, 4, 4, 4], P('section', None, 'expert'), may hold values from 0 to 3, as said below
- keep: int32 [4, 4], replicated, may hold values 0 or 1
Outputs:
- grads: bfloat16 [4, 4, 64, 4096], P('section', None, 'expert', 'mp')
Inputs may be any that keep to these rules, and one draw needn't show every extreme that they name: Each row assign[l, m, i, :] names every expert exactly 1 times.
All inputs are finite; a program needn't handle non-finite values.
Results may differ from a plain program's by a relative error of at most 0.017.
Values may be sent and summed in bfloat16 or wider, within the bound.
A program may use at most 128 MiB of HBM per device.

v0:
```python
import jax
import jax.numpy as jnp
from jax import lax
from jax.sharding import PartitionSpec as P

PER = 1


def shifted(value, axis, by):
    peers = lax.axis_size(axis)
    pairs = [(i, i + by) for i in range(peers) if 0 <= i + by < peers]
    return lax.ppermute(value, axis, pairs)


def body(grad_top, w_down, w_up, saved, assign, keep):
    n_section = lax.axis_size("section")
    n_expert = lax.axis_size("expert")
    section_index = lax.axis_index("section")
    tiles_dev = assign.shape[-1]
    experts = tiles_dev // PER
    group_size = n_expert // experts
    micro_count = grad_top.shape[0]
    token_rows = grad_top.shape[1]
    width = grad_top.shape[2]
    tile_rows = token_rows // tiles_dev
    slab_rows = PER * tile_rows
    down_projection = w_down[0, 0]
    up_proj = w_up[0, 0]
    stored = saved[0, :, 0]
    routes = assign[0, :, 0]
    rows_e = stored.shape[1]
    results = jnp.zeros((micro_count, token_rows, width), jnp.bfloat16)
    incoming = jnp.zeros((token_rows, width), jnp.bfloat16)
    steps_total = micro_count + n_section - 1
    for turn in range(steps_total):
        raw_index = turn - (n_section - 1) + section_index
        active = (raw_index >= 0) & (raw_index < micro_count)
        micro_index = jnp.clip(raw_index, 0, micro_count - 1)
        top_grad = lax.dynamic_index_in_dim(grad_top, micro_index, 0, keepdims=False)
        current = jnp.where(section_index == n_section - 1, top_grad, incoming)
        route_row = lax.dynamic_index_in_dim(routes, micro_index, 0, keepdims=False)
        onehot = (route_row[:, None] == jnp.arange(experts, dtype=jnp.int32)[None, :]).astype(
            jnp.int32
        )
        before = jnp.cumsum(onehot, axis=0) - onehot
        tile_rank = jnp.sum(before * onehot, axis=1)
        position_index = route_row * PER + tile_rank
        placing = (
            position_index[None, :] == jnp.arange(tiles_dev, dtype=jnp.int32)[:, None]
        ).astype(jnp.bfloat16)
        ordered = jnp.dot(
            placing,
            current.reshape(tiles_dev, tile_rows * width),
            preferred_element_type=jnp.float32,
        ).astype(jnp.bfloat16)
        outgoing = jnp.broadcast_to(
            ordered.reshape(experts, 1, slab_rows, width), (experts, group_size, slab_rows, width)
        )
        outgoing = outgoing.reshape(n_expert, slab_rows, width)
        arrived = lax.all_to_all(
            outgoing, "expert", split_axis=0, concat_axis=0, tiled=True
        ).reshape(rows_e, width)
        partial_value = lax.dot_general(
            arrived, down_projection, (((1,), (1,)), ((), ())), preferred_element_type=jnp.float32
        )
        pre_act = lax.dynamic_index_in_dim(stored, micro_index, 0, keepdims=False)
        expert_share_total = lax.psum_scatter(
            partial_value.astype(jnp.bfloat16), "mp", scatter_dimension=0, tiled=True
        ).astype(jnp.float32)
        share_rows = rows_e // lax.axis_size("mp")
        own_rows = lax.dynamic_slice_in_dim(
            pre_act, lax.axis_index("mp") * share_rows, share_rows, 0
        )
        local_grad = jnp.where(own_rows > 0, expert_share_total, 0.0).astype(jnp.bfloat16)
        hidden_grad = lax.all_gather(local_grad, "mp", axis=0, tiled=True)
        back_part = lax.dot_general(
            hidden_grad, up_proj, (((1,), (1,)), ((), ())), preferred_element_type=jnp.float32
        ).astype(jnp.bfloat16)
        returned = lax.all_to_all(
            back_part.reshape(n_expert, slab_rows, width),
            "expert",
            split_axis=0,
            concat_axis=0,
            tiled=True,
        )
        summed = jnp.sum(
            returned.reshape(experts, group_size, slab_rows, width), axis=1, dtype=jnp.float32
        )
        row_updates = jnp.take(summed, position_index, axis=0).reshape(token_rows, width)
        factor = keep[section_index, micro_index].astype(jnp.float32)
        fresh_grad = (current.astype(jnp.float32) + factor * row_updates).astype(jnp.bfloat16)
        previous = lax.dynamic_index_in_dim(results, micro_index, 0, keepdims=False)
        results = lax.dynamic_update_index_in_dim(
            results, jnp.where(active, fresh_grad, previous), micro_index, 0
        )
        if turn + 1 < steps_total:
            incoming = shifted(fresh_grad, "section", -1)
    return results[None]


def solution(mesh):
    placed = (
        P(None, "expert", "mp"),
        P("section", "expert", None, "mp"),
        P("section", "expert", "mp", None),
        P("section", None, "expert", None, None),
        P("section", None, "expert", None),
        P(),
    )
    return jax.shard_map(
        body,
        mesh=mesh,
        in_specs=placed,
        out_specs=P("section", None, "expert", "mp"),
        check_vma=False,
    )
```

profile of v0, /device:TPU:0, one launch (start us, length us, event | category | flops | bytes accessed | tf_op | source)
XLA Modules:
  0.0 438.2 jit_solution(9176409022689948413)
XLA Ops:
  9.5 6.3 %all-to-all-start = ((bf16[4,4,2048]{2,1,0:T(4,128)(2,1)}), bf16[4,4,2048]{2,1,0:T(4,128)(2,1)S(1)}, u32[]{:S(2)}, u32[]{:S(2)}) async-start(bf16[4,4,2048]{2,1,0:T(4,128)(2,1)} %reshape_reshape.21), calls=%async_computation | async-start | bytes 131072 | tf_op jit(solution)/shard_map/all_to_all | solution.py:60
  16.1 5.4 %all-to-all-done = bf16[4,4,2048]{2,1,0:T(4,128)(2,1)S(1)} async-done(((bf16[4,4,2048]{2,1,0:T(4,128)(2,1)}), bf16[4,4,2048]{2,1,0:T(4,128)(2,1)S(1)}, u32[]{:S(2)}, u32[]{:S(2)}) %all-to-all-start) | async-done | bytes 65568 | tf_op jit(solution)/shard_map/all_to_all | solution.py:60
  21.6 10.9 %fusion.28 = bf16[16,4096]{1,0:T(8,128)(2,1)} fusion(bf16[16,2048]{1,0:T(8,128)(2,1)S(1)} %reshape.258, bf16[1,1,4096,2048]{3,2,1,0:T(8,128)(2,1)} %param.9), kind=kOutput, calls=%fused_computation.42 | convolution fusion | flops 268500992 | bytes 16973824 | tf_op jit(solution)/shard_map/dot_general | solution.py:63
  34.5 7.1 %reduce-scatter.8.cloned.1.call-done = bf16[8,4096]{1,0:T(8,128)(2,1)} async-done(((bf16[16,4096]{1,0:T(8,128)(2,1)}), bf16[8,4096]{1,0:T(8,128)(2,1)}) %reduce-scatter.8.cloned.1.call-update) | async-done | bytes 65552 | tf_op jit(solution)/shard_map/reduce_scatter | solution.py:67
  42.5 4.9 %all_gather.21 = bf16[16,4096]{1,0:T(8,128)(2,1)S(1)} all-gather(bf16[8,4096]{1,0:T(8,128)(2,1)S(1)} %select_convert_fusion.6), channel_id=1, replica_groups=mesh['section'=4,'expert'=4,'mp'=2] {'mp'}, dimensions={0}, use_global_device_ids=true | all-gather | bytes 196608 | tf_op jit(solution)/shard_map/all_gather | solution.py:75
  47.4 10.2 %fusion.49 = bf16[16,2048]{1,0:T(8,128)(2,1)S(1)} fusion(bf16[16,4096]{1,0:T(8,128)(2,1)S(1)} %all_gather.21, bf16[1,1,2048,4096]{3,2,1,0:T(8,128)(2,1)} %param.10), kind=kOutput, calls=%fused_computation.49 | convolution fusion | flops 268468224 | bytes 16973824 | tf_op jit(solution)/shard_map/dot_general | solution.py:76
  58.3 4.6 %all-to-all-start.1 = ((bf16[4,4,2048]{2,1,0:T(4,128)(2,1)}), bf16[4,4,2048]{2,1,0:T(4,128)(2,1)S(1)}, u32[]{:S(2)}, u32[]{:S(2)}) async-start(bf16[4,4,2048]{2,1,0:T(4,128)(2,1)} %reshape.259), calls=%async_computation.2 | async-start | bytes 131072 | tf_op jit(solution)/shard_map/all_to_all | solution.py:79
  62.9 5.7 %all-to-all-done.1 = bf16[4,4,2048]{2,1,0:T(4,128)(2,1)S(1)} async-done(((bf16[4,4,2048]{2,1,0:T(4,128)(2,1)}), bf16[4,4,2048]{2,1,0:T(4,128)(2,1)S(1)}, u32[]{:S(2)}, u32[]{:S(2)}) %all-to-all-start.1) | async-done | bytes 65568 | tf_op jit(solution)/shard_map/all_to_all | solution.py:79
  77.2 5.4 %all-to-all-done.2 = bf16[4,4,2048]{2,1,0:T(4,128)(2,1)S(1)} async-done(((bf16[4,4,2048]{2,1,0:T(4,128)(2,1)}), bf16[4,4,2048]{2,1,0:T(4,128)(2,1)S(1)}, u32[]{:S(2)}, u32[]{:S(2)}) %all-to-all-start.2) | async-done | bytes 65568 | tf_op jit(solution)/shard_map/all_to_all | solution.py:60
  82.6 10.9 %fusion.31 = bf16[16,4096]{1,0:T(8,128)(2,1)} fusion(bf16[16,2048]{1,0:T(8,128)(2,1)S(1)} %reshape.261, bf16[1,1,4096,2048]{3,2,1,0:T(8,128)(2,1)} %param.9), kind=kOutput, calls=%fused_computation.43 | convolution fusion | flops 268500992 | bytes 16973824 | tf_op jit(solution)/shard_map/dot_general | solution.py:63
  93.6 8.7 %reduce-scatter.10.cloned.1.call-done = bf16[8,4096]{1,0:T(8,128)(2,1)} async-done(((bf16[16,4096]{1,0:T(8,128)(2,1)}), bf16[8,4096]{1,0:T(8,128)(2,1)}) %reduce-scatter.10.cloned.1.call-update) | async-done | bytes 65552 | tf_op jit(solution)/shard_map/reduce_scatter | solution.py:67
  103.2 4.9 %all_gather.22 = bf16[16,4096]{1,0:T(8,128)(2,1)S(1)} all-gather(bf16[8,4096]{1,0:T(8,128)(2,1)S(1)} %select_convert_fusion.5), channel_id=1, replica_groups=mesh['section'=4,'expert'=4,'mp'=2] {'mp'}, dimensions={0}, use_global_device_ids=true | all-gather | bytes 196608 | tf_op jit(solution)/shard_map/all_gather | solution.py:75
  108.1 10.2 %fusion.52 = bf16[16,2048]{1,0:T(8,128)(2,1)S(1)} fusion(bf16[16,4096]{1,0:T(8,128)(2,1)S(1)} %all_gather.22, bf16[1,1,2048,4096]{3,2,1,0:T(8,128)(2,1)} %param.10), kind=kOutput, calls=%fused_computation.50 | convolution fusion | flops 268468224 | bytes 16973824 | tf_op jit(solution)/shard_map/dot_general | solution.py:76
  119.0 4.6 %all-to-all-start.3 = ((bf16[4,4,2048]{2,1,0:T(4,128)(2,1)}), bf16[4,4,2048]{2,1,0:T(4,128)(2,1)S(1)}, u32[]{:S(2)}, u32[]{:S(2)}) async-start(bf16[4,4,2048]{2,1,0:T(4,128)(2,1)} %reshape.262), calls=%async_computation.5 | async-start | bytes 131072 | tf_op jit(solution)/shard_map/all_to_all | solution.py:79
  123.6 5.7 %all-to-all-done.3 = bf16[4,4,2048]{2,1,0:T(4,128)(2,1)S(1)} async-done(((bf16[4,4,2048]{2,1,0:T(4,128)(2,1)}), bf16[4,4,2048]{2,1,0:T(4,128)(2,1)S(1)}, u32[]{:S(2)}, u32[]{:S(2)}) %all-to-all-start.3) | async-done | bytes 65568 | tf_op jit(solution)/shard_map/all_to_all | solution.py:79
  137.7 5.6 %all-to-all-done.4 = bf16[4,4,2048]{2,1,0:T(4,128)(2,1)S(1)} async-done(((bf16[4,4,2048]{2,1,0:T(4,128)(2,1)}), bf16[4,4,2048]{2,1,0:T(4,128)(2,1)S(1)}, u32[]{:S(2)}, u32[]{:S(2)}) %all-to-all-start.4) | async-done | bytes 65568 | tf_op jit(solution)/shard_map/all_to_all | solution.py:60
  143.3 10.9 %fusion.34 = bf16[16,4096]{1,0:T(8,128)(2,1)} fusion(bf16[16,2048]{1,0:T(8,128)(2,1)S(1)} %reshape.264, bf16[1,1,4096,2048]{3,2,1,0:T(8,128)(2,1)} %param.9), kind=kOutput, calls=%fused_computation.44 | convolution fusion | flops 268500992 | bytes 16973824 | tf_op jit(solution)/shard_map/dot_general | solution.py:63
  155.1 7.9 %reduce-scatter.12.cloned.1.call-done = bf16[8,4096]{1,0:T(8,128)(2,1)} async-done(((bf16[16,4096]{1,0:T(8,128)(2,1)}), bf16[8,4096]{1,0:T(8,128)(2,1)}) %reduce-scatter.12.cloned.1.call-update) | async-done | bytes 65552 | tf_op jit(solution)/shard_map/reduce_scatter | solution.py:67
  163.8 5.3 %all_gather.23 = bf16[16,4096]{1,0:T(8,128)(2,1)S(1)} all-gather(bf16[8,4096]{1,0:T(8,128)(2,1)S(1)} %select_convert_fusion.4), channel_id=1, replica_groups=mesh['section'=4,'expert'=4,'mp'=2] {'mp'}, dimensions={0}, use_global_device_ids=true | all-gather | bytes 196608 | tf_op jit(solution)/shard_map/all_gather | solution.py:75
  169.1 10.2 %fusion.55 = bf16[16,2048]{1,0:T(8,128)(2,1)S(1)} fusion(bf16[16,4096]{1,0:T(8,128)(2,1)S(1)} %all_gather.23, bf16[1,1,2048,4096]{3,2,1,0:T(8,128)(2,1)} %param.10), kind=kOutput, calls=%fused_computation.51 | convolution fusion | flops 268468224 | bytes 16973824 | tf_op jit(solution)/shard_map/dot_general | solution.py:76
  180.0 4.6 %all-to-all-start.5 = ((bf16[4,4,2048]{2,1,0:T(4,128)(2,1)}), bf16[4,4,2048]{2,1,0:T(4,128)(2,1)S(1)}, u32[]{:S(2)}, u32[]{:S(2)}) async-start(bf16[4,4,2048]{2,1,0:T(4,128)(2,1)} %reshape.265), calls=%async_computation.8 | async-start | bytes 131072 | tf_op jit(solution)/shard_map/all_to_all | solution.py:79
  184.6 5.7 %all-to-all-done.5 = bf16[4,4,2048]{2,1,0:T(4,128)(2,1)S(1)} async-done(((bf16[4,4,2048]{2,1,0:T(4,128)(2,1)}), bf16[4,4,2048]{2,1,0:T(4,128)(2,1)S(1)}, u32[]{:S(2)}, u32[]{:S(2)}) %all-to-all-start.5) | async-done | bytes 65568 | tf_op jit(solution)/shard_map/all_to_all | solution.py:79
  194.7 8.1 %all_to_all.70 = bf16[4,4,2048]{2,1,0:T(4,128)(2,1)S(1)} all-to-all(bf16[4,4,2048]{2,1,0:T(4,128)(2,1)S(1)} %reshape_reshape.24), channel_id=1, replica_groups=mesh['section'=4,'expert'=4,'mp'=2] {'expert'}, dimensions={0} | all-to-all | bytes 131072 | tf_op jit(solution)/shard_map/all_to_all | solution.py:60
  202.8 10.9 %fusion.37 = bf16[16,4096]{1,0:T(8,128)(2,1)} fusion(bf16[16,2048]{1,0:T(8,128)(2,1)S(1)} %reshape.267, bf16[1,1,4096,2048]{3,2,1,0:T(8,128)(2,1)} %param.9), kind=kOutput, calls=%fused_computation.45 | convolution fusion | flops 268500992 | bytes 16973824 | tf_op jit(solution)/shard_map/dot_general | solution.py:63
  214.5 8.0 %reduce-scatter.14.cloned.1.call-done = bf16[8,4096]{1,0:T(8,128)(2,1)} async-done(((bf16[16,4096]{1,0:T(8,128)(2,1)}), bf16[8,4096]{1,0:T(8,128)(2,1)}) %reduce-scatter.14.cloned.1.call-update) | async-done | bytes 65552 | tf_op jit(solution)/shard_map/reduce_scatter | solution.py:67
  223.4 5.1 %all_gather.24 = bf16[16,4096]{1,0:T(8,128)(2,1)S(1)} all-gather(bf16[8,4096]{1,0:T(8,128)(2,1)S(1)} %select_convert_fusion.3), channel_id=1, replica_groups=mesh['section'=4,'expert'=4,'mp'=2] {'mp'}, dimensions={0}, use_global_device_ids=true | all-gather | bytes 196608 | tf_op jit(solution)/shard_map/all_gather | solution.py:75
  228.5 10.2 %fusion.58 = bf16[16,2048]{1,0:T(8,128)(2,1)S(1)} fusion(bf16[16,4096]{1,0:T(8,128)(2,1)S(1)} %all_gather.24, bf16[1,1,2048,4096]{3,2,1,0:T(8,128)(2,1)} %param.10), kind=kOutput, calls=%fused_computation.52 | convolution fusion | flops 268468224 | bytes 16973824 | tf_op jit(solution)/shard_map/dot_general | solution.py:76
  243.9 5.7 %all-to-all-done.7 = bf16[4,4,2048]{2,1,0:T(4,128)(2,1)S(1)} async-done(((bf16[4,4,2048]{2,1,0:T(4,128)(2,1)}), bf16[4,4,2048]{2,1,0:T(4,128)(2,1)S(1)}, u32[]{:S(2)}, u32[]{:S(2)}) %all-to-all-start.7) | async-done | bytes 65568 | tf_op jit(solution)/shard_map/all_to_all | solution.py:79
  258.0 5.6 %all-to-all-done.8 = bf16[4,4,2048]{2,1,0:T(4,128)(2,1)S(1)} async-done(((bf16[4,4,2048]{2,1,0:T(4,128)(2,1)}), bf16[4,4,2048]{2,1,0:T(4,128)(2,1)S(1)}, u32[]{:S(2)}, u32[]{:S(2)}) %all-to-all-start.8) | async-done | bytes 65568 | tf_op jit(solution)/shard_map/all_to_all | solution.py:60
  263.6 10.9 %fusion.40 = bf16[16,4096]{1,0:T(8,128)(2,1)} fusion(bf16[16,2048]{1,0:T(8,128)(2,1)S(1)} %reshape.270, bf16[1,1,4096,2048]{3,2,1,0:T(8,128)(2,1)} %param.9), kind=kOutput, calls=%fused_computation.46 | convolution fusion | flops 268500992 | bytes 16973824 | tf_op jit(solution)/shard_map/dot_general | solution.py:63
  275.4 7.9 %reduce-scatter.16.cloned.1.call-done = bf16[8,4096]{1,0:T(8,128)(2,1)} async-done(((bf16[16,4096]{1,0:T(8,128)(2,1)}), bf16[8,4096]{1,0:T(8,128)(2,1)}) %reduce-scatter.16.cloned.1.call-update) | async-done | bytes 65552 | tf_op jit(solution)/shard_map/reduce_scatter | solution.py:67
  284.2 5.1 %all_gather.25 = bf16[16,4096]{1,0:T(8,128)(2,1)S(1)} all-gather(bf16[8,4096]{1,0:T(8,128)(2,1)S(1)} %select_convert_fusion.2), channel_id=1, replica_groups=mesh['section'=4,'expert'=4,'mp'=2] {'mp'}, dimensions={0}, use_global_device_ids=true | all-gather | bytes 196608 | tf_op jit(solution)/shard_map/all_gather | solution.py:75
  289.3 10.2 %fusion.61 = bf16[16,2048]{1,0:T(8,128)(2,1)S(1)} fusion(bf16[16,4096]{1,0:T(8,128)(2,1)S(1)} %all_gather.25, bf16[1,1,2048,4096]{3,2,1,0:T(8,128)(2,1)} %param.10), kind=kOutput, calls=%fused_computation.53 | convolution fusion | flops 268468224 | bytes 16973824 | tf_op jit(solution)/shard_map/dot_general | solution.py:76
  300.2 4.6 %all-to-all-start.9 = ((bf16[4,4,2048]{2,1,0:T(4,128)(2,1)}), bf16[4,4,2048]{2,1,0:T(4,128)(2,1)S(1)}, u32[]{:S(2)}, u32[]{:S(2)}) async-start(bf16[4,4,2048]{2,1,0:T(4,128)(2,1)} %reshape.271), calls=%async_computation.14 | async-start | bytes 131072 | tf_op jit(solution)/shard_map/all_to_all | solution.py:79
  304.8 5.7 %all-to-all-done.9 = bf16[4,4,2048]{2,1,0:T(4,128)(2,1)S(1)} async-done(((bf16[4,4,2048]{2,1,0:T(4,128)(2,1)}), bf16[4,4,2048]{2,1,0:T(4,128)(2,1)S(1)}, u32[]{:S(2)}, u32[]{:S(2)}) %all-to-all-start.9) | async-done | bytes 65568 | tf_op jit(solution)/shard_map/all_to_all | solution.py:79
  314.9 8.1 %all_to_all.71 = bf16[4,4,2048]{2,1,0:T(4,128)(2,1)S(1)} all-to-all(bf16[4,4,2048]{2,1,0:T(4,128)(2,1)S(1)} %reshape_reshape.26), channel_id=1, replica_groups=mesh['section'=4,'expert'=4,'mp'=2] {'expert'}, dimensions={0} | all-to-all | bytes 131072 | tf_op jit(solution)/shard_map/all_to_all | solution.py:60
  323.0 10.9 %fusion.43 = bf16[16,4096]{1,0:T(8,128)(2,1)} fusion(bf16[16,2048]{1,0:T(8,128)(2,1)S(1)} %reshape.273, bf16[1,1,4096,2048]{3,2,1,0:T(8,128)(2,1)} %param.9), kind=kOutput, calls=%fused_computation.47 | convolution fusion | flops 268500992 | bytes 16973824 | tf_op jit(solution)/shard_map/dot_general | solution.py:63
  334.8 7.9 %reduce-scatter.18.cloned.1.call-done = bf16[8,4096]{1,0:T(8,128)(2,1)} async-done(((bf16[16,4096]{1,0:T(8,128)(2,1)}), bf16[8,4096]{1,0:T(8,128)(2,1)}) %reduce-scatter.18.cloned.1.call-update) | async-done | bytes 65552 | tf_op jit(solution)/shard_map/reduce_scatter | solution.py:67
  343.6 5.2 %all_gather.26 = bf16[16,4096]{1,0:T(8,128)(2,1)S(1)} all-gather(bf16[8,4096]{1,0:T(8,128)(2,1)S(1)} %select_convert_fusion.1), channel_id=1, replica_groups=mesh['section'=4,'expert'=4,'mp'=2] {'mp'}, dimensions={0}, use_global_device_ids=true | all-gather | bytes 196608 | tf_op jit(solution)/shard_map/all_gather | solution.py:75
  348.7 10.2 %fusion.64 = bf16[16,2048]{1,0:T(8,128)(2,1)S(1)} fusion(bf16[16,4096]{1,0:T(8,128)(2,1)S(1)} %all_gather.26, bf16[1,1,2048,4096]{3,2,1,0:T(8,128)(2,1)} %param.10), kind=kOutput, calls=%fused_computation.54 | convolution fusion | flops 268468224 | bytes 16973824 | tf_op jit(solution)/shard_map/dot_general | solution.py:76
  359.6 4.6 %all-to-all-start.11 = ((bf16[4,4,2048]{2,1,0:T(4,128)(2,1)}), bf16[4,4,2048]{2,1,0:T(4,128)(2,1)S(1)}, u32[]{:S(2)}, u32[]{:S(2)}) async-start(bf16[4,4,2048]{2,1,0:T(4,128)(2,1)} %reshape.274), calls=%async_computation.17 | async-start | bytes 131072 | tf_op jit(solution)/shard_map/all_to_all | solution.py:79
  364.2 5.7 %all-to-all-done.11 = bf16[4,4,2048]{2,1,0:T(4,128)(2,1)S(1)} async-done(((bf16[4,4,2048]{2,1,0:T(4,128)(2,1)}), bf16[4,4,2048]{2,1,0:T(4,128)(2,1)S(1)}, u32[]{:S(2)}, u32[]{:S(2)}) %all-to-all-start.11) | async-done | bytes 65568 | tf_op jit(solution)/shard_map/all_to_all | solution.py:79
  374.3 8.1 %all_to_all.72 = bf16[4,4,2048]{2,1,0:T(4,128)(2,1)S(1)} all-to-all(bf16[4,4,2048]{2,1,0:T(4,128)(2,1)S(1)} %reshape_reshape.27), channel_id=1, replica_groups=mesh['section'=4,'expert'=4,'mp'=2] {'expert'}, dimensions={0} | all-to-all | bytes 131072 | tf_op jit(solution)/shard_map/all_to_all | solution.py:60
  382.4 10.9 %fusion.46 = bf16[16,4096]{1,0:T(8,128)(2,1)} fusion(bf16[16,2048]{1,0:T(8,128)(2,1)S(1)} %reshape.276, bf16[1,1,4096,2048]{3,2,1,0:T(8,128)(2,1)} %param.9), kind=kOutput, calls=%fused_computation.48 | convolution fusion | flops 268500992 | bytes 16973824 | tf_op jit(solution)/shard_map/dot_general | solution.py:63
  394.0 8.1 %reduce-scatter.20.cloned.1.call-done = bf16[8,4096]{1,0:T(8,128)(2,1)} async-done(((bf16[16,4096]{1,0:T(8,128)(2,1)}), bf16[8,4096]{1,0:T(8,128)(2,1)}) %reduce-scatter.20.cloned.1.call-update) | async-done | bytes 65552 | tf_op jit(solution)/shard_map/reduce_scatter | solution.py:67
  402.9 5.2 %all_gather.27 = bf16[16,4096]{1,0:T(8,128)(2,1)S(1)} all-gather(bf16[8,4096]{1,0:T(8,128)(2,1)S(1)} %select_convert_fusion), channel_id=1, replica_groups=mesh['section'=4,'expert'=4,'mp'=2] {'mp'}, dimensions={0}, use_global_device_ids=true | all-gather | bytes 196608 | tf_op jit(solution)/shard_map/all_gather | solution.py:75
  408.2 10.2 %fusion.67 = bf16[16,2048]{1,0:T(8,128)(2,1)S(1)} fusion(bf16[16,4096]{1,0:T(8,128)(2,1)S(1)} %all_gather.27, bf16[1,1,2048,4096]{3,2,1,0:T(8,128)(2,1)} %param.10), kind=kOutput, calls=%fused_computation.55 | convolution fusion | flops 268468224 | bytes 16973824 | tf_op jit(solution)/shard_map/dot_general | solution.py:76
  424.3 5.0 %all-to-all-done.13 = bf16[4,4,2048]{2,1,0:T(4,128)(2,1)S(1)} async-done(((bf16[4,4,2048]{2,1,0:T(4,128)(2,1)}), bf16[4,4,2048]{2,1,0:T(4,128)(2,1)S(1)}, u32[]{:S(2)}, u32[]{:S(2)}) %all-to-all-start.13) | async-done | bytes 65568 | tf_op jit(solution)/shard_map/all_to_all | solution.py:79
  (171 shorter events, 65.3 us)
Async XLA Ops:
  6.5 26.0 %copy-start.2 = (s32[4,4]{1,0:T(4,128)S(1)}, s32[4,4]{1,0:T(4,128)}, u32[]{:S(2)}) copy-start(s32[4,4]{1,0:T(4,128)} %param.13) | copy-start | bytes 196
  6.5 35.1 %copy-start.1 = (bf16[1,4,1,16,4096]{4,3,2,1,0:T(8,128)(2,1)S(1)}, bf16[1,4,1,16,4096]{4,3,2,1,0:T(8,128)(2,1)}, u32[]{:S(2)}) copy-start(bf16[1,4,1,16,4096]{4,3,2,1,0:T(8,128)(2,1)} %param.11) | copy-start | bytes 1572868
  9.5 12.1 %all-to-all-start = ((bf16[4,4,2048]{2,1,0:T(4,128)(2,1)}), bf16[4,4,2048]{2,1,0:T(4,128)(2,1)S(1)}, u32[]{:S(2)}, u32[]{:S(2)}) async-start(bf16[4,4,2048]{2,1,0:T(4,128)(2,1)} %reshape_reshape.21), calls=%async_computation | async-start | bytes 131072 | tf_op jit(solution)/shard_map/all_to_all | solution.py:60
  15.8 25.8 %reduce-scatter.8.cloned.1.call-start = ((), (), s32[]{:S(2)}) async-start(), calls=%async_computation.21 | async-start | bytes 196608 | tf_op jit(solution)/shard_map/reduce_scatter | solution.py:67
  21.6 47.9 %copy-start = (bf16[4,16,2048]{2,1,0:T(8,128)(2,1)S(1)}, bf16[4,16,2048]{2,1,0:T(8,128)(2,1)}, u32[]{:S(2)}) copy-start(bf16[4,16,2048]{2,1,0:T(8,128)(2,1)} %param.8) | copy-start | bytes 786436
  58.3 10.3 %all-to-all-start.1 = ((bf16[4,4,2048]{2,1,0:T(4,128)(2,1)}), bf16[4,4,2048]{2,1,0:T(4,128)(2,1)S(1)}, u32[]{:S(2)}, u32[]{:S(2)}) async-start(bf16[4,4,2048]{2,1,0:T(4,128)(2,1)} %reshape.259), calls=%async_computation.2 | async-start | bytes 131072 | tf_op jit(solution)/shard_map/all_to_all | solution.py:79
  69.5 3.1 collective-permute-start
  73.6 9.0 %all-to-all-start.2 = ((bf16[4,4,2048]{2,1,0:T(4,128)(2,1)}), bf16[4,4,2048]{2,1,0:T(4,128)(2,1)S(1)}, u32[]{:S(2)}, u32[]{:S(2)}) async-start(bf16[4,4,2048]{2,1,0:T(4,128)(2,1)} %reshape_reshape.22), calls=%async_computation.3 | async-start | bytes 131072 | tf_op jit(solution)/shard_map/all_to_all | solution.py:60
  76.9 25.4 %reduce-scatter.10.cloned.1.call-start = ((), (), s32[]{:S(2)}) async-start(), calls=%async_computation.22 | async-start | bytes 196608 | tf_op jit(solution)/shard_map/reduce_scatter | solution.py:67
  119.0 10.4 %all-to-all-start.3 = ((bf16[4,4,2048]{2,1,0:T(4,128)(2,1)}), bf16[4,4,2048]{2,1,0:T(4,128)(2,1)S(1)}, u32[]{:S(2)}, u32[]{:S(2)}) async-start(bf16[4,4,2048]{2,1,0:T(4,128)(2,1)} %reshape.262), calls=%async_computation.5 | async-start | bytes 131072 | tf_op jit(solution)/shard_map/all_to_all | solution.py:79
  130.2 3.1 collective-permute-start.1
  134.3 9.0 %all-to-all-start.4 = ((bf16[4,4,2048]{2,1,0:T(4,128)(2,1)}), bf16[4,4,2048]{2,1,0:T(4,128)(2,1)S(1)}, u32[]{:S(2)}, u32[]{:S(2)}) async-start(bf16[4,4,2048]{2,1,0:T(4,128)(2,1)} %reshape_reshape.23), calls=%async_computation.6 | async-start | bytes 131072 | tf_op jit(solution)/shard_map/all_to_all | solution.py:60
  137.5 25.4 %reduce-scatter.12.cloned.1.call-start = ((), (), s32[]{:S(2)}) async-start(), calls=%async_computation.23 | async-start | bytes 196608 | tf_op jit(solution)/shard_map/reduce_scatter | solution.py:67
  180.0 10.4 %all-to-all-start.5 = ((bf16[4,4,2048]{2,1,0:T(4,128)(2,1)}), bf16[4,4,2048]{2,1,0:T(4,128)(2,1)S(1)}, u32[]{:S(2)}, u32[]{:S(2)}) async-start(bf16[4,4,2048]{2,1,0:T(4,128)(2,1)} %reshape.265), calls=%async_computation.8 | async-start | bytes 131072 | tf_op jit(solution)/shard_map/all_to_all | solution.py:79
  184.6 37.9 %reduce-scatter.14.cloned.1.call-start = ((), (), s32[]{:S(2)}) async-start(), calls=%async_computation.24 | async-start | bytes 196608 | tf_op jit(solution)/shard_map/reduce_scatter | solution.py:67
  191.2 3.1 collective-permute-start.2
  239.4 10.3 %all-to-all-start.7 = ((bf16[4,4,2048]{2,1,0:T(4,128)(2,1)}), bf16[4,4,2048]{2,1,0:T(4,128)(2,1)S(1)}, u32[]{:S(2)}, u32[]{:S(2)}) async-start(bf16[4,4,2048]{2,1,0:T(4,128)(2,1)} %reshape.268), calls=%async_computation.11 | async-start | bytes 131072 | tf_op jit(solution)/shard_map/all_to_all | solution.py:79
  250.5 3.1 collective-permute-start.3
  254.6 9.0 %all-to-all-start.8 = ((bf16[4,4,2048]{2,1,0:T(4,128)(2,1)}), bf16[4,4,2048]{2,1,0:T(4,128)(2,1)S(1)}, u32[]{:S(2)}, u32[]{:S(2)}) async-start(bf16[4,4,2048]{2,1,0:T(4,128)(2,1)} %reshape_reshape.25), calls=%async_computation.12 | async-start | bytes 131072 | tf_op jit(solution)/shard_map/all_to_all | solution.py:60
  257.9 25.4 %reduce-scatter.16.cloned.1.call-start = ((), (), s32[]{:S(2)}) async-start(), calls=%async_computation.25 | async-start | bytes 196608 | tf_op jit(solution)/shard_map/reduce_scatter | solution.py:67
  300.2 10.4 %all-to-all-start.9 = ((bf16[4,4,2048]{2,1,0:T(4,128)(2,1)}), bf16[4,4,2048]{2,1,0:T(4,128)(2,1)S(1)}, u32[]{:S(2)}, u32[]{:S(2)}) async-start(bf16[4,4,2048]{2,1,0:T(4,128)(2,1)} %reshape.271), calls=%async_computation.14 | async-start | bytes 131072 | tf_op jit(solution)/shard_map/all_to_all | solution.py:79
  304.8 37.9 %reduce-scatter.18.cloned.1.call-start = ((), (), s32[]{:S(2)}) async-start(), calls=%async_computation.26 | async-start | bytes 196608 | tf_op jit(solution)/shard_map/reduce_scatter | solution.py:67
  311.4 3.1 collective-permute-start.4
  359.6 10.4 %all-to-all-start.11 = ((bf16[4,4,2048]{2,1,0:T(4,128)(2,1)}), bf16[4,4,2048]{2,1,0:T(4,128)(2,1)S(1)}, u32[]{:S(2)}, u32[]{:S(2)}) async-start(bf16[4,4,2048]{2,1,0:T(4,128)(2,1)} %reshape.274), calls=%async_computation.17 | async-start | bytes 131072 | tf_op jit(solution)/shard_map/all_to_all | solution.py:79
  364.2 37.8 %reduce-scatter.20.cloned.1.call-start = ((), (), s32[]{:S(2)}) async-start(), calls=%async_computation.27 | async-start | bytes 196608 | tf_op jit(solution)/shard_map/reduce_scatter | solution.py:67
  370.8 3.1 collective-permute-start.5
  419.0 10.3 %all-to-all-start.13 = ((bf16[4,4,2048]{2,1,0:T(4,128)(2,1)}), bf16[4,4,2048]{2,1,0:T(4,128)(2,1)S(1)}, u32[]{:S(2)}, u32[]{:S(2)}) async-start(bf16[4,4,2048]{2,1,0:T(4,128)(2,1)} %reshape.277), calls=%async_computation.20 | async-start | bytes 131072 | tf_op jit(solution)/shard_map/all_to_all | solution.py:79
Sparse Core Ops, SparseCore 0:
  32.6 8.9 reduce-scatter.7
  93.6 8.6 reduce-scatter.9
  154.3 8.5 reduce-scatter.11
  213.8 8.6 reduce-scatter.13
  274.7 8.5 reduce-scatter.15
  334.0 8.6 reduce-scatter.17
  393.4 8.5 reduce-scatter.19
where the time goes:
time: 447 us; the launch traced here: 438 us
  matrix products  149 us (33%)
  waiting for transfers between devices  128 us (29%)
  blocking collectives  60.2 us (13%)
  starting transfers between devices  56.5 us (13%)
  between operations  19 us (4%)
  local copies, waits for them, and re-layouts  15.4 us (3%)
  other arithmetic  10.7 us (2%)
    dot_general x7, matrix products, body(): lax.dot_general(arrived, down_projection, (((1,), (1,)), ((), ())), prefe...  76.1 us
    dot_general x7, matrix products, body(): lax.dot_general(hidden_grad, up_proj, (((1,), (1,)), ((), ())), preferred...  71.3 us
    reduce_scatter x7, waiting for transfers between devices, body(): lax.psum_scatter(partial_value.astype(jnp.bfloat16), 'mp', scatter_dimens...  55.5 us
    all_to_all x7, waiting for transfers between devices, body(): lax.all_to_all(back_part.reshape(n_expert, slab_rows, width), 'expert', s...  39.4 us
    all_gather x7, blocking collectives, body(): hidden_grad = lax.all_gather(local_grad, 'mp', axis=0, tiled=True)  35.9 us
    all_to_all x7, starting transfers between devices, body(): lax.all_to_all(back_part.reshape(n_expert, slab_rows, width), 'expert', s...  32.2 us
    all_to_all x3, blocking collectives, body(): lax.all_to_all(outgoing, 'expert', split_axis=0, concat_axis=0, tiled=True)  24.3 us
    all_to_all x4, waiting for transfers between devices, body(): lax.all_to_all(outgoing, 'expert', split_axis=0, concat_axis=0, tiled=True)  22 us
  transfers between devices with their start and end apart: 24, of which 24 were waited for; matrix products, arithmetic and copies ran while one was open for 1% of the time, Pallas kernels for 0%

commit v1 on v0

--- a/solution.py
+++ b/solution.py
@@ -1,9 +1,217 @@
+import functools
+
 import jax
 import jax.numpy as jnp
 from jax import lax
+from jax.experimental import pallas as pl
+from jax.experimental.pallas import tpu as pltpu
 from jax.sharding import PartitionSpec as P
 
 PER = 1
+MESH = pl.DeviceIdType.MESH
+NT = (((1,), (1,)), ((), ()))
+CHUNKS = 4
+
+
+def window_kernel(
+    n_section, n_expert,
+    top_ref, down_hbm, up_hbm, saved_ref, place_ref, back_ref, out_ref,
+    down, up, cur, incoming, send_a, recv_a, send_b, recv_b, mp_send, mp_recv,
+    rows, gathered, own, hidden,
+    w_sem, a_send, a_recv, b_send, b_recv, m_send, m_recv, s_send, s_recv,
+):
+    s = lax.axis_index("section")
+    e = lax.axis_index("expert")
+    x = lax.axis_index("mp")
+    micro = top_ref.shape[0]
+    slab = send_a.shape[2]
+    ff = down.shape[0]
+    width = up.shape[0]
+    fc, wc = ff // CHUNKS, width // CHUNKS
+    down_copy = pltpu.make_async_copy(down_hbm, down, w_sem.at[0])
+    up_copy = pltpu.make_async_copy(up_hbm, up, w_sem.at[1])
+    down_copy.start()
+    up_copy.start()
+
+    barrier = pltpu.get_barrier_semaphore()
+    for d in range(1, n_expert):
+        pl.semaphore_signal(
+            barrier, inc=1, device_id={"expert": lax.rem(e + d, n_expert)}, device_id_type=MESH
+        )
+    pl.semaphore_signal(barrier, inc=1, device_id={"mp": 1 - x}, device_id_type=MESH)
+    for d in (1, n_section - 1):
+        pl.semaphore_signal(
+            barrier, inc=1, device_id={"section": lax.rem(s + d, n_section)}, device_id_type=MESH
+        )
+    pl.semaphore_wait(barrier, n_expert + 2)
+
+    def tile_copy(m, d, src, dst, send_sem, recv_sem):
+        peer = lax.rem(e + d, n_expert)
+        return pltpu.make_async_remote_copy(
+            src_ref=src.at[m, peer],
+            dst_ref=dst.at[m, e],
+            send_sem=send_sem.at[m, d],
+            recv_sem=recv_sem.at[m, e],
+            device_id={"expert": peer},
+            device_id_type=MESH,
+        )
+
+    def tile_arrival(m, d, src, dst, send_sem, recv_sem):
+        peer = lax.rem(e + d, n_expert)
+        return pltpu.make_async_remote_copy(
+            src_ref=src.at[m, peer],
+            dst_ref=dst.at[m, peer],
+            send_sem=send_sem.at[m, d],
+            recv_sem=recv_sem.at[m, peer],
+            device_id={"expert": peer},
+            device_id_type=MESH,
+        )
+
+    def exchange(m, src, dst, send_sem, recv_sem):
+        for k in range(n_expert):
+            src[m, k] = rows[k * slab : (k + 1) * slab, :].astype(jnp.bfloat16)
+        for d in range(1, n_expert):
+            tile_copy(m, d, src, dst, send_sem, recv_sem).start()
+        dst[m, e] = src[m, e]
+        for d in range(1, n_expert):
+            tile_arrival(m, d, src, dst, send_sem, recv_sem).wait_recv()
+        for k in range(n_expert):
+            gathered[k * slab : (k + 1) * slab, :] = dst[m, k].astype(jnp.float32)
+        return gathered[...].astype(jnp.bfloat16)
+
+    def mp_copy(m, c):
+        return pltpu.make_async_remote_copy(
+            src_ref=mp_send.at[m, c],
+            dst_ref=mp_recv.at[m, c],
+            send_sem=m_send.at[m, c],
+            recv_sem=m_recv.at[m, c],
+            device_id={"mp": 1 - x},
+            device_id_type=MESH,
+        )
+
+    def section_copy(m):
+        return pltpu.make_async_remote_copy(
+            src_ref=out_ref.at[m],
+            dst_ref=incoming.at[m],
+            send_sem=s_send.at[m],
+            recv_sem=s_recv.at[m],
+            device_id={"section": lax.rem(s + n_section - 1, n_section)},
+            device_id_type=MESH,
+        )
+
+    def step(m, carry):
+        @pl.when(s == n_section - 1)
+        def _():
+            cur[...] = top_ref[m]
+
+        @pl.when(s < n_section - 1)
+        def _():
+            section_copy(m).wait_recv()
+            cur[...] = incoming[m]
+
+        rows[...] = jnp.dot(place_ref[m], cur[...], preferred_element_type=jnp.float32)
+        arrived = exchange(m, send_a, recv_a, a_send, a_recv)
+
+        @pl.when(m == 0)
+        def _():
+            down_copy.wait()
+
+        for c in range(CHUNKS):
+            part = lax.dot_general(
+                arrived, down[c * fc : (c + 1) * fc, :], NT, preferred_element_type=jnp.float32
+            )
+            own[:, c * fc : (c + 1) * fc] = part
+            mp_send[m, c] = part.astype(jnp.bfloat16)
+            mp_copy(m, c).start()
+        for c in range(CHUNKS):
+            mp_copy(m, c).wait_recv()
+            total = own[:, c * fc : (c + 1) * fc] + mp_recv[m, c].astype(jnp.float32)
+            gate = saved_ref[m, :, c * fc : (c + 1) * fc].astype(jnp.float32)
+            hidden[:, c * fc : (c + 1) * fc] = jnp.where(gate > 0, total, 0.0).astype(jnp.bfloat16)
+
+        @pl.when(m == 0)
+        def _():
+            up_copy.wait()
+
+        for c in range(CHUNKS):
+            rows[:, c * wc : (c + 1) * wc] = lax.dot_general(
+                hidden[...], up[c * wc : (c + 1) * wc, :], NT, preferred_element_type=jnp.float32
+            )
+        returned = exchange(m, send_b, recv_b, b_send, b_recv)
+        update = jnp.dot(back_ref[m], returned, preferred_element_type=jnp.float32)
+        out_ref[m] = (cur[...].astype(jnp.float32) + update).astype(jnp.bfloat16)
+
+        @pl.when(s > 0)
+        def _():
+            section_copy(m).start()
+
+        for d in range(1, n_expert):
+            tile_copy(m, d, send_a, recv_a, a_send, a_recv).wait_send()
+            tile_copy(m, d, send_b, recv_b, b_send, b_recv).wait_send()
+        for c in range(CHUNKS):
+            mp_copy(m, c).wait_send()
+        return carry
+
+    lax.fori_loop(0, micro, step, 0)
+
+    @pl.when(s > 0)
+    def _():
+        for m in range(micro):
+            section_copy(m).wait_send()
+
+
+def fused(grad_top, w_down, w_up, saved, assign, keep):
+    n_section = lax.axis_size("section")
+    n_expert = lax.axis_size("expert")
+    micro, tokens, width = grad_top.shape
+    ff = w_down.shape[2]
+    tiles = assign.shape[-1]
+    tile_rows = tokens // tiles
+    slab = PER * tile_rows
+    routes = assign[0, :, 0]
+    factor = lax.dynamic_index_in_dim(keep, lax.axis_index("section"), 0, keepdims=False)
+    spot = jnp.repeat(routes, tile_rows, axis=1) * tile_rows + jnp.arange(tokens, dtype=jnp.int32) % tile_rows
+    ids = jnp.arange(tokens, dtype=jnp.int32)
+    place = (spot[:, None, :] == ids[None, :, None]).astype(jnp.bfloat16)
+    back = ((spot[:, :, None] == ids[None, None, :]) & (factor[:, None, None] > 0)).astype(jnp.bfloat16)
+    bf, f32, dma = jnp.bfloat16, jnp.float32, pltpu.SemaphoreType.DMA
+    vm = pl.BlockSpec(memory_space=pltpu.VMEM)
+    hbm = pl.BlockSpec(memory_space=pl.ANY)
+    out = pl.pallas_call(
+        functools.partial(window_kernel, n_section, n_expert),
+        out_shape=jax.ShapeDtypeStruct((micro, tokens, width), bf),
+        in_specs=[vm, hbm, hbm, vm, vm, vm],
+        out_specs=vm,
+        scratch_shapes=[
+            pltpu.VMEM((ff, width), bf),
+            pltpu.VMEM((width, ff), bf),
+            pltpu.VMEM((tokens, width), bf),
+            pltpu.VMEM((micro, tokens, width), bf),
+            pltpu.VMEM((micro, n_expert, slab, width), bf),
+            pltpu.VMEM((micro, n_expert, slab, width), bf),
+            pltpu.VMEM((micro, n_expert, slab, width), bf),
+            pltpu.VMEM((micro, n_expert, slab, width), bf),
+            pltpu.VMEM((micro, CHUNKS, tokens, ff // CHUNKS), bf),
+            pltpu.VMEM((micro, CHUNKS, tokens, ff // CHUNKS), bf),
+            pltpu.VMEM((tokens, width), f32),
+            pltpu.VMEM((tokens, width), f32),
+            pltpu.VMEM((tokens, ff), f32),
+            pltpu.VMEM((tokens, ff), bf),
+            dma((2,)),
+            dma((micro, n_expert)),
+            dma((micro, n_expert)),
+            dma((micro, n_expert)),
+            dma((micro, n_expert)),
+            dma((micro, CHUNKS)),
+            dma((micro, CHUNKS)),
+            dma((micro,)),
+            dma((micro,)),
+        ],
+        compiler_params=pltpu.CompilerParams(
+            collective_id=0, has_side_effects=True, vmem_limit_bytes=60 * 1024 * 1024
+        ),
+    )(grad_top, w_down[0, 0], w_up[0, 0], saved[0, :, 0], place, back)
+    return out[None]
 
 
 def shifted(value, axis, by):
@@ -107,8 +315,15 @@
         P("section", None, "expert", None),
         P(),
     )
+    whole_experts = mesh.shape["expert"] == 4 and mesh.shape["mp"] == 2 and mesh.shape["section"] == 4
+
+    def choose(grad_top, w_down, w_up, saved, assign, keep):
+        one_each = assign.shape[-1] == mesh.shape["expert"] and PER == 1
+        form = fused if whole_experts and one_each else body
+        return form(grad_top, w_down, w_up, saved, assign, keep)
+
     return jax.shard_map(
-        body,
+        choose,
         mesh=mesh,
         in_specs=placed,
         out_specs=P("section", None, "expert", "mp"),

time: 447 us -> 154 us (0.34); the launches traced: 438 us -> 154 us
  Pallas kernels: 0 us -> 150 us
  matrix products: 149 us -> 0 us
  waiting for transfers between devices: 128 us -> 0 us
  blocking collectives: 60.2 us -> 0 us
  starting transfers between devices: 56.5 us -> 0 us
  between operations: 19 us -> 0.01 us
  local copies, waits for them, and re-layouts: 15.4 us -> 1.83 us
  other arithmetic: 10.7 us -> 2.08 us
    pallas_call x0 -> x1, Pallas kernels: none -> 150 us  [fused(): pl.pallas_call(functools.partial(window_kernel, n_section, n_expert), out...]
    dot_general x21 -> x0, matrix products: 149 us -> none  [the longest x7 76.1 us: body(): lax.dot_general(arrived, down_projection, (((1,), (1,)), ((), ())), prefe...]
    all_to_all x11 -> x0, waiting for transfers between devices: 61.4 us -> none  [the longest x7 39.4 us: body(): lax.all_to_all(back_part.reshape(n_expert, slab_rows, width), 'expert', s...]
    reduce_scatter x7 -> x0, waiting for transfers between devices: 55.5 us -> none  [body(): lax.psum_scatter(partial_value.astype(jnp.bfloat16), 'mp', scatter_dimens...]
    all_to_all x11 -> x0, starting transfers between devices: 48.4 us -> none  [the longest x7 32.2 us: body(): lax.all_to_all(back_part.reshape(n_expert, slab_rows, width), 'expert', s...]
    all_gather x7 -> x0, blocking collectives: 35.9 us -> none  [body(): hidden_grad = lax.all_gather(local_grad, 'mp', axis=0, tiled=True)]
    all_to_all x3 -> x0, blocking collectives: 24.3 us -> none  [body(): lax.all_to_all(outgoing, 'expert', split_axis=0, concat_axis=0, tiled=True)]
    ppermute x6 -> x0, waiting for transfers between devices: 10.8 us -> none  [shifted(): return lax.ppermute(value, axis, pairs)]
  transfers between devices with their start and end apart: 24 -> 0, of which waited for: 24 -> 0; matrix products, arithmetic and copies ran while one was open for 1% -> 0% of each run, Pallas kernels for 0% -> 0%
where the time goes in v1:
time: 154 us
  Pallas kernels  150 us (97%)
  other arithmetic  2.08 us (1%)
  local copies, waits for them, and re-layouts  1.83 us (1%)
    pallas_call x1, Pallas kernels, fused(): pl.pallas_call(functools.partial(window_kernel, n_section, n_expert), out...  150 us

profile of v1, /device:TPU:0, one launch (start us, length us, event | category | flops | bytes accessed | tf_op | source)
XLA Modules:
  0.0 153.7 jit_solution(10551926975095451088)
XLA Ops:
  0.0 0.7 compare_bitcast_fusion
  0.7 0.7 broadcast_multiply_fusion
  1.4 0.1 broadcast_in_dim.4
  1.5 0.1 mul.24
  1.5 0.7 fusion.2
  2.2 149.8 %shard_map.64 = bf16[4,16,2048]{2,1,0:T(8,128)(2,1)} custom-call(bf16[4,16,2048]{2,1,0:T(8,128)(2,1)} %top_ref.1, bf16[4096,2048]{1,0:T(8,128)(2,1)} %bitcast.7, bf16[2048,4096]{1,0:T(8,128)(2,1)} %bitcast.8, bf16[4,16,4096]{2,1,0:T(8,128)(2,1)} %bitcast.10, bf16[4,16,16]{2,1,0:T(8,128)(2,1)} %get-tuple-element.6.place_ref, ...), custom_call_target="tpu_custom_call" | custom-call | tf_op jit(solution)/shard_map/pallas_call | solution.py:180
  152.0 1.7 %copy.8 = bf16[1,4,16,2048]{3,2,1,0:T(8,128)(2,1)} copy(bf16[1,4,16,2048]{3,2,1,0:T(8,128)(2,1)} %bitcast.9) | data formatting | bytes 524288
  (2 shorter events, 0.0 us)
